TPU v7x, 256 devices: a whole 4x4x8 slice. The times are simulated.
256 devices in a mesh: pipe: 8 (over z), seq: 16 (over x, y), tp: 2 (over core).
Axes of the slice: x: 4, y: 4, z: 8, core: 2. Of those that a mesh axis runs over, the one named last changes fastest.
Arguments:
- layer_inputs: bfloat16 [8, 2048, 4096], P('pipe', ('seq', 'tp')), may hold values from -6 to 6
- out_grad: bfloat16 [2048, 4096], P('seq', 'tp'), may hold values from -6 to 6
- short_weights: bfloat16 [8, 7, 3, 4096], P('pipe', None, None, 'tp'), may hold values from -2 to 2
- long_filters: bfloat16 [8, 256, 128], P('pipe', 'tp'), may hold values from -0.15625 to 0.15625
- out_weights: bfloat16 [8, 4096, 4096], P('pipe', 'tp', 'seq'), may hold values from -0.09375 to 0.09375
Outputs:
- input_grad: bfloat16 [8, 2048, 4096], P('pipe', 'seq', 'tp')
- short_grad: float32 [8, 7, 3, 4096], P('pipe', None, None, 'tp')
- long_grad: float32 [8, 256, 128], P('pipe', 'tp')
All inputs are finite; a program needn't handle non-finite values.
Results may differ from a plain program's by a relative error of at most 0.03.
Values may be sent and summed in bfloat16 or wider, within the bound.
No kernel may reach another device: no remote copies, remote signals or barrier semaphores. Data moves between devices by JAX's collectives and lax.ppermute only.
A program may use at most 192 MiB of HBM per device.

v0:
```python
import jax
import jax.numpy as jnp
from jax import lax
from jax.sharding import PartitionSpec as P


def passed_along(array, axis, by):
    size = lax.axis_size(axis)
    pairs = [(i, i + by) for i in range(size) if 0 <= i + by < size]
    return lax.ppermute(array, axis, pairs)


def toeplitz_blocks(filters):
    groups, kernel_width = filters.shape
    base_row = jnp.concatenate(
        [
            jnp.zeros((groups, 1), filters.dtype),
            filters[:, ::-1],
            jnp.zeros((groups, kernel_width), filters.dtype),
        ],
        axis=1,
    )
    tiled = jnp.tile(base_row, (1, kernel_width))[:, : 2 * kernel_width * kernel_width]
    return tiled.reshape(groups, kernel_width, 2 * kernel_width)


def lag_sums(products):
    groups, kernel_width, window = products.shape
    flattened = products.reshape(groups, kernel_width * window)
    flattened = jnp.pad(flattened, ((0, 0), (0, kernel_width)))
    skewed = flattened.reshape(groups, kernel_width, window + 1)
    totals = jnp.sum(skewed, axis=1)
    return totals[:, 1 : kernel_width + 1][:, ::-1]


def to_groups(rows, groups):
    count = rows.shape[0]
    return jnp.transpose(rows.reshape(count, groups, rows.shape[1] // groups), (1, 2, 0))


def from_groups(blocks):
    groups, width, count = blocks.shape
    return jnp.transpose(blocks, (2, 0, 1)).reshape(count, groups * width)


def featurize(source, weights):
    tap_count = weights.shape[0]
    row_count = source.shape[0] - tap_count + 1
    running = jnp.zeros((weights.shape[1], row_count, source.shape[1]), jnp.float32)
    for offset in range(tap_count):
        start = tap_count - 1 - offset
        running = running + weights[offset][:, None, :] * source[start : start + row_count][None]
    return running


def spread_back(feature_grads, weights):
    tap_count = weights.shape[0]
    row_count = feature_grads.shape[1] - tap_count + 1
    running = jnp.zeros((row_count, feature_grads.shape[2]), jnp.float32)
    for offset in range(tap_count):
        running = running + jnp.sum(
            weights[offset][:, None, :] * feature_grads[:, offset : offset + row_count], axis=0
        )
    return running


def weight_grads(feature_grads, source):
    row_count = feature_grads.shape[1]
    tap_count = source.shape[0] - row_count + 1
    terms = []
    for offset in range(tap_count):
        start = tap_count - 1 - offset
        terms.append(jnp.sum(feature_grads * source[start : start + row_count][None], axis=1))
    return jnp.stack(terms)


def long_forward(padded, toeplitz, groups):
    grouped = to_groups(padded, groups)
    result = jnp.einsum("gis,gcs->gci", toeplitz, grouped, preferred_element_type=jnp.float32)
    return from_groups(result)


def long_backward(trailing, reversed_band, groups):
    grouped = to_groups(trailing, groups)
    result = jnp.einsum("grj,gcr->gcj", reversed_band, grouped, preferred_element_type=jnp.float32)
    return from_groups(result)


def filter_grads(mixed_grad, padded, groups):
    grad_groups = to_groups(mixed_grad, groups)
    value_groups = to_groups(padded, groups)
    products = jnp.einsum(
        "gci,gcs->gis", grad_groups, value_groups, preferred_element_type=jnp.float32
    )
    return lag_sums(products)


def recompute(layer_block, weights, filters):
    local_rows = lax.all_to_all(layer_block, "tp", split_axis=1, concat_axis=0, tiled=True)
    tap_count = weights.shape[0]
    kernel_width = filters.shape[1]
    before = passed_along(local_rows[local_rows.shape[0] - tap_count + 1 :], "seq", 1)
    extended = jnp.concatenate([before, local_rows], axis=0).astype(jnp.float32)
    features = featurize(extended, weights)
    products = (features[1] * features[2]).astype(jnp.bfloat16)
    earlier_products = passed_along(products[products.shape[0] - kernel_width + 1 :], "seq", 1)
    padded = jnp.concatenate(
        [jnp.zeros((1, products.shape[1]), jnp.bfloat16), earlier_products, products], axis=0
    )
    toeplitz = toeplitz_blocks(filters)
    reversed_band = jnp.concatenate(
        [toeplitz[:, :, kernel_width:], toeplitz[:, :, :kernel_width]], axis=1
    )
    mixed_rows = long_forward(padded, toeplitz, filters.shape[0])
    return (features, padded, reversed_band, mixed_rows, extended)


def dense_grad(incoming, columns, active):
    empty_sum = jnp.zeros((incoming.shape[0], columns.shape[0]), jnp.float32)
    piece = lax.all_gather(incoming, "tp", axis=1, tiled=True)
    summed = lax.cond(
        active,
        lambda: jnp.einsum("td,cd->tc", piece, columns, preferred_element_type=jnp.float32),
        lambda: empty_sum,
    )
    return summed.astype(jnp.bfloat16)


def backward(saved_state, incoming, dense_part, weights, groups, active):
    features, padded, reversed_band, mixed_rows, source = saved_state
    tap_count = weights.shape[0]
    kernel_width = reversed_band.shape[2]
    token_count, channels = incoming.shape
    edge_rows = tap_count - 1
    dense_float = dense_part.astype(jnp.float32)
    mixed_grad = (dense_float * features[0]).astype(jnp.bfloat16)
    after_grad = passed_along(mixed_grad[: kernel_width - 1], "seq", -1)
    trailing_grad = jnp.concatenate(
        [mixed_grad, after_grad, jnp.zeros((1, channels), jnp.bfloat16)], axis=0
    )

    def middle(operand):
        product_grad = long_backward(operand, reversed_band, groups)
        query_grad = dense_float * mixed_rows
        return (
            jnp.stack([query_grad, product_grad * features[2], product_grad * features[1]]),
            product_grad,
        )

    def middle_skipped(operand):
        return (
            jnp.zeros((3, token_count, channels), jnp.float32),
            jnp.zeros((token_count, channels), jnp.float32),
        )

    feature_grads, product_grad = lax.cond(active, middle, middle_skipped, trailing_grad)
    head_zeros = jnp.zeros((3, edge_rows, channels), jnp.float32)
    partial_sums = spread_back(
        jnp.concatenate([head_zeros, feature_grads[:, :edge_rows]], axis=1), weights
    )
    overflow = passed_along(partial_sums.astype(jnp.bfloat16), "seq", -1).astype(partial_sums.dtype)

    def finish(operands):
        grads, spill = operands
        trailing = jnp.concatenate([grads, head_zeros], axis=1)
        tail_rows = jnp.concatenate(
            [jnp.zeros((token_count - edge_rows, channels), jnp.float32), spill], axis=0
        )
        total = incoming.astype(jnp.float32) + spread_back(trailing, weights) + tail_rows
        return total.astype(jnp.bfloat16)

    def finish_skipped(operands):
        return jnp.zeros((token_count, channels), jnp.bfloat16)

    return (lax.cond(active, finish, finish_skipped, (feature_grads, overflow)), product_grad)


def per_device(layer_inputs, out_grad, short_weights, long_filters, out_weights):
    sections = lax.axis_size("pipe")
    section_index = lax.axis_index("pipe")
    weights = short_weights[0].astype(jnp.float32)
    filters = long_filters[0]
    groups = filters.shape[0]
    saved_state = recompute(layer_inputs[0], weights, filters)
    features, padded, reversed_band, mixed_rows, source = saved_state
    columns = lax.all_gather(out_weights[0], "seq", axis=1, tiled=True)
    incoming = out_grad
    input_result = jnp.zeros_like(out_grad)
    dense_kept = jnp.zeros(out_grad.shape, jnp.bfloat16)
    product_kept = jnp.zeros(out_grad.shape, jnp.float32)
    for step_index in range(sections):
        active = section_index == sections - 1 - step_index
        dense_part = dense_grad(incoming, columns, active)
        input_grad, product_grad = backward(
            saved_state, incoming, dense_part, weights, groups, active
        )
        input_result = jnp.where(active, input_grad, input_result)
        dense_kept = jnp.where(active, dense_part, dense_kept)
        product_kept = jnp.where(active, product_grad, product_kept)
        if step_index + 1 < sections:
            incoming = passed_along(input_grad, "pipe", -1)
    dense_float = dense_kept.astype(jnp.float32)
    mixed_grad = (dense_float * features[0]).astype(jnp.bfloat16)
    feature_grads = jnp.stack(
        [dense_float * mixed_rows, product_kept * features[2], product_kept * features[1]]
    )
    short_local = weight_grads(feature_grads, source)
    long_local = filter_grads(mixed_grad, padded, groups)
    short_result, long_result = (
        lax.psum(short_local.astype(jnp.bfloat16), "seq").astype(jnp.float32),
        lax.psum(long_local.astype(jnp.bfloat16), "seq").astype(jnp.float32),
    )
    return (input_result[None], short_result[None], long_result[None])


def solution(mesh):
    in_specs = (
        P("pipe", ("seq", "tp"), None),
        P("seq", "tp"),
        P("pipe", None, None, "tp"),
        P("pipe", "tp", None),
        P("pipe", "tp", "seq"),
    )
    out_specs = (P("pipe", "seq", "tp"), P("pipe", None, None, "tp"), P("pipe", "tp", None))
    return jax.shard_map(
        per_device, mesh=mesh, in_specs=in_specs, out_specs=out_specs, check_vma=False
    )
```

profile of v0, /device:TPU:32, one launch (start us, length us, event | category | flops | bytes accessed | tf_op | source)
XLA Modules:
  0.0 1389.2 jit_solution(17497464794075836733)
XLA Ops:
  22.8 13.0 tile.10
  42.9 12.5 copy.273
  88.4 68.1 %all-gather.27.cloned.1.call-done = bf16[1,2048,4096]{2,1,0:T(8,128)(2,1)} async-done(((bf16[1,2048,256]{2,1,0:T(8,128)(2,1)}), bf16[1,2048,4096]{2,1,0:T(8,128)(2,1)}) %all-gather.27.cloned.1.call-update) | async-done | bytes 16777232 | tf_op jit(solution)/shard_map/all_gather | solution.py:186
  197.7 9.4 multiply_reduce_fusion.110
  208.8 12.2 collective-permute-done.3
  225.3 10.5 collective-permute-done.4
  235.9 56.1 %all-gather.13.cloned.1.call-done = bf16[128,4096]{1,0:T(8,128)(2,1)} async-done(((bf16[128,2048]{1,0:T(8,128)(2,1)}), bf16[128,4096]{1,0:T(8,128)(2,1)}) %all-gather.13.cloned.1.call-update) | async-done | bytes 1048592 | tf_op jit(solution)/shard_map/all_gather | solution.py:120
  298.1 14.7 %collective-permute-done.5 = bf16[127,2048]{0,1:T(8,128)(2,1)S(1)} collective-permute-done((bf16[127,2048]{0,1:T(8,128)(2,1)S(1)}, bf16[127,2048]{0,1:T(8,128)(2,1)S(1)}, u32[]{:S(2)}, u32[]{:S(2)}) %collective-permute-start.5) | collective-permute-done | bytes 520224 | tf_op jit(solution)/shard_map/ppermute | solution.py:10
  319.0 9.7 multiply_reduce_fusion.104
  330.3 13.9 %collective-permute-done.6 = bf16[6,2048]{0,1:T(8,128)(2,1)S(1)} collective-permute-done((bf16[6,2048]{0,1:T(8,128)(2,1)S(1)}, bf16[6,2048]{0,1:T(8,128)(2,1)S(1)}, u32[]{:S(2)}, u32[]{:S(2)}) %collective-permute-start.6) | collective-permute-done | bytes 24608 | tf_op jit(solution)/shard_map/ppermute | solution.py:10
  349.0 12.0 collective-permute-done.7
  361.0 63.3 %all-gather.15.cloned.1.call-done = bf16[128,4096]{1,0:T(8,128)(2,1)} async-done(((bf16[128,2048]{1,0:T(8,128)(2,1)}), bf16[128,4096]{1,0:T(8,128)(2,1)}) %all-gather.15.cloned.1.call-update) | async-done | bytes 1048592 | tf_op jit(solution)/shard_map/all_gather | solution.py:120
  430.1 14.7 %collective-permute-done.8 = bf16[127,2048]{0,1:T(8,128)(2,1)S(1)} collective-permute-done((bf16[127,2048]{0,1:T(8,128)(2,1)S(1)}, bf16[127,2048]{0,1:T(8,128)(2,1)S(1)}, u32[]{:S(2)}, u32[]{:S(2)}) %collective-permute-start.8) | collective-permute-done | bytes 520224 | tf_op jit(solution)/shard_map/ppermute | solution.py:10
  451.2 9.7 multiply_reduce_fusion.98
  462.6 13.9 %collective-permute-done.9 = bf16[6,2048]{0,1:T(8,128)(2,1)S(1)} collective-permute-done((bf16[6,2048]{0,1:T(8,128)(2,1)S(1)}, bf16[6,2048]{0,1:T(8,128)(2,1)S(1)}, u32[]{:S(2)}, u32[]{:S(2)}) %collective-permute-start.9) | collective-permute-done | bytes 24608 | tf_op jit(solution)/shard_map/ppermute | solution.py:10
  481.0 12.0 collective-permute-done.10
  493.1 64.1 %all-gather.17.cloned.1.call-done = bf16[128,4096]{1,0:T(8,128)(2,1)} async-done(((bf16[128,2048]{1,0:T(8,128)(2,1)}), bf16[128,4096]{1,0:T(8,128)(2,1)}) %all-gather.17.cloned.1.call-update) | async-done | bytes 1048592 | tf_op jit(solution)/shard_map/all_gather | solution.py:120
  562.9 14.7 %collective-permute-done.11 = bf16[127,2048]{0,1:T(8,128)(2,1)S(1)} collective-permute-done((bf16[127,2048]{0,1:T(8,128)(2,1)S(1)}, bf16[127,2048]{0,1:T(8,128)(2,1)S(1)}, u32[]{:S(2)}, u32[]{:S(2)}) %collective-permute-start.11) | collective-permute-done | bytes 520224 | tf_op jit(solution)/shard_map/ppermute | solution.py:10
  584.3 9.7 multiply_reduce_fusion.92
  595.6 13.9 %collective-permute-done.12 = bf16[6,2048]{0,1:T(8,128)(2,1)S(1)} collective-permute-done((bf16[6,2048]{0,1:T(8,128)(2,1)S(1)}, bf16[6,2048]{0,1:T(8,128)(2,1)S(1)}, u32[]{:S(2)}, u32[]{:S(2)}) %collective-permute-start.12) | collective-permute-done | bytes 24608 | tf_op jit(solution)/shard_map/ppermute | solution.py:10
  614.1 12.0 collective-permute-done.13
  626.1 65.0 %all-gather.19.cloned.1.call-done = bf16[128,4096]{1,0:T(8,128)(2,1)} async-done(((bf16[128,2048]{1,0:T(8,128)(2,1)}), bf16[128,4096]{1,0:T(8,128)(2,1)}) %all-gather.19.cloned.1.call-update) | async-done | bytes 1048592 | tf_op jit(solution)/shard_map/all_gather | solution.py:120
  696.9 14.7 %collective-permute-done.14 = bf16[127,2048]{0,1:T(8,128)(2,1)S(1)} collective-permute-done((bf16[127,2048]{0,1:T(8,128)(2,1)S(1)}, bf16[127,2048]{0,1:T(8,128)(2,1)S(1)}, u32[]{:S(2)}, u32[]{:S(2)}) %collective-permute-start.14) | collective-permute-done | bytes 520224 | tf_op jit(solution)/shard_map/ppermute | solution.py:10
  717.9 9.7 multiply_reduce_fusion.86
  729.2 13.9 %collective-permute-done.15 = bf16[6,2048]{0,1:T(8,128)(2,1)S(1)} collective-permute-done((bf16[6,2048]{0,1:T(8,128)(2,1)S(1)}, bf16[6,2048]{0,1:T(8,128)(2,1)S(1)}, u32[]{:S(2)}, u32[]{:S(2)}) %collective-permute-start.15) | collective-permute-done | bytes 24608 | tf_op jit(solution)/shard_map/ppermute | solution.py:10
  747.9 12.0 collective-permute-done.16
  759.9 64.0 %all-gather.21.cloned.1.call-done = bf16[128,4096]{1,0:T(8,128)(2,1)} async-done(((bf16[128,2048]{1,0:T(8,128)(2,1)}), bf16[128,4096]{1,0:T(8,128)(2,1)}) %all-gather.21.cloned.1.call-update) | async-done | bytes 1048592 | tf_op jit(solution)/shard_map/all_gather | solution.py:120
  829.6 14.7 %collective-permute-done.17 = bf16[127,2048]{0,1:T(8,128)(2,1)S(1)} collective-permute-done((bf16[127,2048]{0,1:T(8,128)(2,1)S(1)}, bf16[127,2048]{0,1:T(8,128)(2,1)S(1)}, u32[]{:S(2)}, u32[]{:S(2)}) %collective-permute-start.17) | collective-permute-done | bytes 520224 | tf_op jit(solution)/shard_map/ppermute | solution.py:10
  850.9 9.7 multiply_reduce_fusion.80
  862.3 13.9 %collective-permute-done.18 = bf16[6,2048]{0,1:T(8,128)(2,1)S(1)} collective-permute-done((bf16[6,2048]{0,1:T(8,128)(2,1)S(1)}, bf16[6,2048]{0,1:T(8,128)(2,1)S(1)}, u32[]{:S(2)}, u32[]{:S(2)}) %collective-permute-start.18) | collective-permute-done | bytes 24608 | tf_op jit(solution)/shard_map/ppermute | solution.py:10
  880.8 57.0 %collective-permute-done.19 = bf16[128,2048]{1,0:T(8,128)(2,1)} collective-permute-done((bf16[128,2048]{1,0:T(8,128)(2,1)}, bf16[128,2048]{1,0:T(8,128)(2,1)}, u32[]{:S(2)}, u32[]{:S(2)}) %collective-permute-start.19) | collective-permute-done | bytes 524320 | tf_op jit(solution)/shard_map/ppermute | solution.py:10
  937.8 16.7 %all-gather.23.cloned.1.call-done = bf16[128,4096]{1,0:T(8,128)(2,1)} async-done(((bf16[128,2048]{1,0:T(8,128)(2,1)}), bf16[128,4096]{1,0:T(8,128)(2,1)}) %all-gather.23.cloned.1.call-update) | async-done | bytes 1048592 | tf_op jit(solution)/shard_map/all_gather | solution.py:120
  954.5 17.2 %conditional.42 = (f32[128,2048]{1,0:T(8,128)}, f32[128,2048]{0,1:T(8,128)}, bf16[128,2048]{0,1:T(8,128)(2,1)}) conditional(s32[]{:T(128)} %convert_element_type.283, () %tuple.255, (bf16[128,4096]{1,0:T(8,128)(2,1)}, bf16[2048,4096]{1,0:T(8,128)(2,1)}) %tuple.637), branch_computations={%region_115.116_spmd, %region_116.117_spmd} | conditional | flops 2148007936 | bytes 22020120 | solution.py:121
  954.5 12.9 fusion.9
  974.4 14.7 %collective-permute-done.20 = bf16[127,2048]{0,1:T(8,128)(2,1)S(1)} collective-permute-done((bf16[127,2048]{0,1:T(8,128)(2,1)S(1)}, bf16[127,2048]{0,1:T(8,128)(2,1)S(1)}, u32[]{:S(2)}, u32[]{:S(2)}) %collective-permute-start.20) | collective-permute-done | bytes 520224 | tf_op jit(solution)/shard_map/ppermute | solution.py:10
  990.5 13.2 conditional.43
  1006.6 9.7 multiply_reduce_fusion.74
  1017.9 13.9 %collective-permute-done.21 = bf16[6,2048]{0,1:T(8,128)(2,1)S(1)} collective-permute-done((bf16[6,2048]{0,1:T(8,128)(2,1)S(1)}, bf16[6,2048]{0,1:T(8,128)(2,1)S(1)}, u32[]{:S(2)}, u32[]{:S(2)}) %collective-permute-start.21) | collective-permute-done | bytes 24608 | tf_op jit(solution)/shard_map/ppermute | solution.py:10
  1032.9 20.9 %conditional.44 = (bf16[128,2048]{1,0:T(8,128)(2,1)}) conditional(s32[]{:T(128)} %convert_element_type.283, () %tuple.217, (bf16[128,2048]{1,0:T(8,128)(2,1)}, f32[7,3,2048]{2,1,0:T(4,128)S(1)}, f32[3,128,2048]{1,2,0:T(8,128)}, f32[6,2048]{0,1:T(8,128)}) %tuple.258), branch_computations={%region_125.126_spmd, %region_126.134_spmd} | conditional | flops 11796480 | bytes 26026020 | solution.py:175
  1039.3 11.9 multiply_reduce_fusion.47
  1055.7 12.7 collective-permute-done.22
  1099.4 17.8 %copy.274 = f32[128,128,256]{0,2,1:T(8,128)} copy(f32[128,128,256]{2,1,0:T(8,128)} %fusion.30) | data formatting | bytes 33554432 | tf_op jit(solution)/shard_map/reshape | solution.py:29
  1117.2 13.3 pad.28
  1130.5 17.5 %reshape.203 = f32[128,128,257]{0,2,1:T(8,128)} reshape(f32[128,32896]{0,1:T(8,128)} %pad.28) | data formatting | bytes 33685504 | tf_op jit(solution)/shard_map/reshape | solution.py:31
  1158.1 77.1 %psum.15 = bf16[1,128,128]{1,2,0:T(8,128)(2,1)} all-reduce(bf16[1,128,128]{1,2,0:T(8,128)(2,1)} %bitcast.399), channel_id=1, replica_groups=mesh['pipe'=8,'seq'=16,'tp'=2] {'seq'}, use_global_device_ids=true, to_apply=%region_162.163 | all-reduce | flops 16384 | bytes 65536 | tf_op jit(solution)/shard_map/psum | solution.py:211
  1256.4 9.4 multiply_reduce_fusion.68
  1268.4 8.9 collective-permute-done.24
  1280.5 99.8 %all-reduce.27.cloned.1.call-done = bf16[1,7,3,2048]{3,1,2,0:T(8,128)(2,1)} async-done(((bf16[1,7,3,2048]{3,1,2,0:T(8,128)(2,1)}), bf16[1,7,3,2048]{3,1,2,0:T(8,128)(2,1)}) %all-reduce.27.cloned.1.call-update) | async-done | bytes 86032 | tf_op jit(solution)/shard_map/psum | solution.py:210
  (283 shorter events, 344.9 us)
Async XLA Ops:
  7.2 10.9 copy-start.64
  7.2 81.3 %all-gather.11.cloned.1.call-start = ((), (), s32[]{:S(2)}) async-start(), calls=%async_computation.1 | async-start | bytes 1572864 | tf_op jit(solution)/shard_map/all_gather | solution.py:120
  7.9 148.7 %all-gather.27.cloned.1.call-start = ((), (), s32[]{:S(2)}) async-start(), calls=%async_computation.10 | async-start | bytes 17825792 | tf_op jit(solution)/shard_map/all_gather | solution.py:186
  8.7 283.3 %all-gather.13.cloned.1.call-start = ((), (), s32[]{:S(2)}) async-start(), calls=%async_computation.2 | async-start | bytes 1572864 | tf_op jit(solution)/shard_map/all_gather | solution.py:120
  14.5 47.9 %collective-permute-start = (bf16[6,2048]{1,0:T(8,128)(2,1)S(1)}, bf16[6,2048]{1,0:T(8,128)(2,1)S(1)}, u32[]{:S(2)}, u32[]{:S(2)}) collective-permute-start(bf16[6,2048]{1,0:T(8,128)(2,1)S(1)} %slice.757), channel_id=1, source_target_pairs={{0,2},{2,4},{4,6},{6,8},{8,10},{10,12},{12,14},{14,16},{16,18},{18... | collective-permute-start | bytes 73736 | tf_op jit(solution)/shard_map/ppermute | solution.py:10
  42.9 12.5 copy-start.63
  70.5 7.7 copy-start.32
  163.8 13.7 collective-permute-start.1
  167.7 14.7 %collective-permute-start.2 = (bf16[127,2048]{0,1:T(8,128)(2,1)}, bf16[127,2048]{0,1:T(8,128)(2,1)}, u32[]{:S(2)}, u32[]{:S(2)}) collective-permute-start(bf16[127,2048]{0,1:T(8,128)(2,1)} %bitcast.344), channel_id=1, source_target_pairs={{2,0},{4,2},{6,4},{8,6},{10,8},{12,10},{14,12},{16,14},{18,16},{20... | collective-permute-start | bytes 1560584 | tf_op jit(solution)/shard_map/ppermute | solution.py:10
  183.2 9.6 slice-start
  185.7 7.1 copy-start.1
  185.8 7.1 slice-start.1
  207.5 13.5 collective-permute-start.3
  222.9 12.9 collective-permute-start.4
  235.8 188.6 %all-gather.15.cloned.1.call-start = ((), (), s32[]{:S(2)}) async-start(), calls=%async_computation.3 | async-start | bytes 1572864 | tf_op jit(solution)/shard_map/all_gather | solution.py:120
  296.8 16.0 %collective-permute-start.5 = (bf16[127,2048]{0,1:T(8,128)(2,1)S(1)}, bf16[127,2048]{0,1:T(8,128)(2,1)S(1)}, u32[]{:S(2)}, u32[]{:S(2)}) collective-permute-start(bf16[127,2048]{0,1:T(8,128)(2,1)S(1)} %bitcast.392), channel_id=1, source_target_pairs={{2,0},{4,2},{6,4},{8,6},{10,8},{12,10},{14,12},{16,14},{18,16},{20... | collective-permute-start | bytes 1560584 | tf_op jit(solution)/shard_map/ppermute | solution.py:10
  316.2 2.8 copy-start.8
  329.0 15.2 %collective-permute-start.6 = (bf16[6,2048]{0,1:T(8,128)(2,1)S(1)}, bf16[6,2048]{0,1:T(8,128)(2,1)S(1)}, u32[]{:S(2)}, u32[]{:S(2)}) collective-permute-start(bf16[6,2048]{0,1:T(8,128)(2,1)S(1)} %add_convert_fusion.14), channel_id=1, source_target_pairs={{2,0},{4,2},{6,4},{8,6},{10,8},{12,10},{14,12},{16,14},{18,16},{20... | collective-permute-start | bytes 73736 | tf_op jit(solution)/shard_map/ppermute | solution.py:10
  346.4 14.6 %collective-permute-start.7 = (bf16[128,2048]{1,0:T(8,128)(2,1)}, bf16[128,2048]{1,0:T(8,128)(2,1)}, u32[]{:S(2)}, u32[]{:S(2)}) collective-permute-start(bf16[128,2048]{1,0:T(8,128)(2,1)} %get-tuple-element.1088), channel_id=1, source_target_pairs={{32,0},{64,32},{96,64},{128,96},{160,128},{192,160},{224,192},{33,... | collective-permute-start | bytes 1572872 | tf_op jit(solution)/shard_map/ppermute | solution.py:10
  361.0 196.2 %all-gather.17.cloned.1.call-start = ((), (), s32[]{:S(2)}) async-start(), calls=%async_computation.4 | async-start | bytes 1572864 | tf_op jit(solution)/shard_map/all_gather | solution.py:120
  428.8 16.0 %collective-permute-start.8 = (bf16[127,2048]{0,1:T(8,128)(2,1)S(1)}, bf16[127,2048]{0,1:T(8,128)(2,1)S(1)}, u32[]{:S(2)}, u32[]{:S(2)}) collective-permute-start(bf16[127,2048]{0,1:T(8,128)(2,1)S(1)} %bitcast.393), channel_id=1, source_target_pairs={{2,0},{4,2},{6,4},{8,6},{10,8},{12,10},{14,12},{16,14},{18,16},{20... | collective-permute-start | bytes 1560584 | tf_op jit(solution)/shard_map/ppermute | solution.py:10
  448.4 2.8 copy-start.11
  461.3 15.2 %collective-permute-start.9 = (bf16[6,2048]{0,1:T(8,128)(2,1)S(1)}, bf16[6,2048]{0,1:T(8,128)(2,1)S(1)}, u32[]{:S(2)}, u32[]{:S(2)}) collective-permute-start(bf16[6,2048]{0,1:T(8,128)(2,1)S(1)} %add_convert_fusion.13), channel_id=1, source_target_pairs={{2,0},{4,2},{6,4},{8,6},{10,8},{12,10},{14,12},{16,14},{18,16},{20... | collective-permute-start | bytes 73736 | tf_op jit(solution)/shard_map/ppermute | solution.py:10
  478.4 14.6 %collective-permute-start.10 = (bf16[128,2048]{1,0:T(8,128)(2,1)}, bf16[128,2048]{1,0:T(8,128)(2,1)}, u32[]{:S(2)}, u32[]{:S(2)}) collective-permute-start(bf16[128,2048]{1,0:T(8,128)(2,1)} %get-tuple-element.1089), channel_id=1, source_target_pairs={{32,0},{64,32},{96,64},{128,96},{160,128},{192,160},{224,192},{33,... | collective-permute-start | bytes 1572872 | tf_op jit(solution)/shard_map/ppermute | solution.py:10
  493.0 198.1 %all-gather.19.cloned.1.call-start = ((), (), s32[]{:S(2)}) async-start(), calls=%async_computation.5 | async-start | bytes 1572864 | tf_op jit(solution)/shard_map/all_gather | solution.py:120
  561.6 16.0 %collective-permute-start.11 = (bf16[127,2048]{0,1:T(8,128)(2,1)S(1)}, bf16[127,2048]{0,1:T(8,128)(2,1)S(1)}, u32[]{:S(2)}, u32[]{:S(2)}) collective-permute-start(bf16[127,2048]{0,1:T(8,128)(2,1)S(1)} %bitcast.394), channel_id=1, source_target_pairs={{2,0},{4,2},{6,4},{8,6},{10,8},{12,10},{14,12},{16,14},{18,16},{20... | collective-permute-start | bytes 1560584 | tf_op jit(solution)/shard_map/ppermute | solution.py:10
  594.3 15.2 %collective-permute-start.12 = (bf16[6,2048]{0,1:T(8,128)(2,1)S(1)}, bf16[6,2048]{0,1:T(8,128)(2,1)S(1)}, u32[]{:S(2)}, u32[]{:S(2)}) collective-permute-start(bf16[6,2048]{0,1:T(8,128)(2,1)S(1)} %add_convert_fusion.12), channel_id=1, source_target_pairs={{2,0},{4,2},{6,4},{8,6},{10,8},{12,10},{14,12},{16,14},{18,16},{20... | collective-permute-start | bytes 73736 | tf_op jit(solution)/shard_map/ppermute | solution.py:10
  611.4 14.6 %collective-permute-start.13 = (bf16[128,2048]{1,0:T(8,128)(2,1)}, bf16[128,2048]{1,0:T(8,128)(2,1)}, u32[]{:S(2)}, u32[]{:S(2)}) collective-permute-start(bf16[128,2048]{1,0:T(8,128)(2,1)} %get-tuple-element.1090), channel_id=1, source_target_pairs={{32,0},{64,32},{96,64},{128,96},{160,128},{192,160},{224,192},{33,... | collective-permute-start | bytes 1572872 | tf_op jit(solution)/shard_map/ppermute | solution.py:10
  626.1 197.9 %all-gather.21.cloned.1.call-start = ((), (), s32[]{:S(2)}) async-start(), calls=%async_computation.6 | async-start | bytes 1572864 | tf_op jit(solution)/shard_map/all_gather | solution.py:120
  695.6 16.0 %collective-permute-start.14 = (bf16[127,2048]{0,1:T(8,128)(2,1)S(1)}, bf16[127,2048]{0,1:T(8,128)(2,1)S(1)}, u32[]{:S(2)}, u32[]{:S(2)}) collective-permute-start(bf16[127,2048]{0,1:T(8,128)(2,1)S(1)} %bitcast.395), channel_id=1, source_target_pairs={{2,0},{4,2},{6,4},{8,6},{10,8},{12,10},{14,12},{16,14},{18,16},{20... | collective-permute-start | bytes 1560584 | tf_op jit(solution)/shard_map/ppermute | solution.py:10
  715.0 2.8 copy-start.17
  727.9 15.2 %collective-permute-start.15 = (bf16[6,2048]{0,1:T(8,128)(2,1)S(1)}, bf16[6,2048]{0,1:T(8,128)(2,1)S(1)}, u32[]{:S(2)}, u32[]{:S(2)}) collective-permute-start(bf16[6,2048]{0,1:T(8,128)(2,1)S(1)} %add_convert_fusion.11), channel_id=1, source_target_pairs={{2,0},{4,2},{6,4},{8,6},{10,8},{12,10},{14,12},{16,14},{18,16},{20... | collective-permute-start | bytes 73736 | tf_op jit(solution)/shard_map/ppermute | solution.py:10
  745.2 14.6 %collective-permute-start.16 = (bf16[128,2048]{1,0:T(8,128)(2,1)}, bf16[128,2048]{1,0:T(8,128)(2,1)}, u32[]{:S(2)}, u32[]{:S(2)}) collective-permute-start(bf16[128,2048]{1,0:T(8,128)(2,1)} %get-tuple-element.1091), channel_id=1, source_target_pairs={{32,0},{64,32},{96,64},{128,96},{160,128},{192,160},{224,192},{33,... | collective-permute-start | bytes 1572872 | tf_op jit(solution)/shard_map/ppermute | solution.py:10
  759.9 194.7 %all-gather.23.cloned.1.call-start = ((), (), s32[]{:S(2)}) async-start(), calls=%async_computation.7 | async-start | bytes 1572864 | tf_op jit(solution)/shard_map/all_gather | solution.py:120
  828.3 16.0 %collective-permute-start.17 = (bf16[127,2048]{0,1:T(8,128)(2,1)S(1)}, bf16[127,2048]{0,1:T(8,128)(2,1)S(1)}, u32[]{:S(2)}, u32[]{:S(2)}) collective-permute-start(bf16[127,2048]{0,1:T(8,128)(2,1)S(1)} %bitcast.396), channel_id=1, source_target_pairs={{2,0},{4,2},{6,4},{8,6},{10,8},{12,10},{14,12},{16,14},{18,16},{20... | collective-permute-start | bytes 1560584 | tf_op jit(solution)/shard_map/ppermute | solution.py:10
  861.0 15.2 %collective-permute-start.18 = (bf16[6,2048]{0,1:T(8,128)(2,1)S(1)}, bf16[6,2048]{0,1:T(8,128)(2,1)S(1)}, u32[]{:S(2)}, u32[]{:S(2)}) collective-permute-start(bf16[6,2048]{0,1:T(8,128)(2,1)S(1)} %add_convert_fusion.10), channel_id=1, source_target_pairs={{2,0},{4,2},{6,4},{8,6},{10,8},{12,10},{14,12},{16,14},{18,16},{20... | collective-permute-start | bytes 73736 | tf_op jit(solution)/shard_map/ppermute | solution.py:10
  878.1 59.6 %collective-permute-start.19 = (bf16[128,2048]{1,0:T(8,128)(2,1)}, bf16[128,2048]{1,0:T(8,128)(2,1)}, u32[]{:S(2)}, u32[]{:S(2)}) collective-permute-start(bf16[128,2048]{1,0:T(8,128)(2,1)} %get-tuple-element.1092), channel_id=1, source_target_pairs={{32,0},{64,32},{96,64},{128,96},{160,128},{192,160},{224,192},{33,... | collective-permute-start | bytes 1572872 | tf_op jit(solution)/shard_map/ppermute | solution.py:10
  937.8 146.2 %all-gather.25.cloned.1.call-start = ((), (), s32[]{:S(2)}) async-start(), calls=%async_computation.8 | async-start | bytes 1572864 | tf_op jit(solution)/shard_map/all_gather | solution.py:120
  973.1 16.0 %collective-permute-start.20 = (bf16[127,2048]{0,1:T(8,128)(2,1)S(1)}, bf16[127,2048]{0,1:T(8,128)(2,1)S(1)}, u32[]{:S(2)}, u32[]{:S(2)}) collective-permute-start(bf16[127,2048]{0,1:T(8,128)(2,1)S(1)} %bitcast.397), channel_id=1, source_target_pairs={{2,0},{4,2},{6,4},{8,6},{10,8},{12,10},{14,12},{16,14},{18,16},{20... | collective-permute-start | bytes 1560584 | tf_op jit(solution)/shard_map/ppermute | solution.py:10
  1003.7 2.8 copy-start.23
  1016.6 15.2 %collective-permute-start.21 = (bf16[6,2048]{0,1:T(8,128)(2,1)S(1)}, bf16[6,2048]{0,1:T(8,128)(2,1)S(1)}, u32[]{:S(2)}, u32[]{:S(2)}) collective-permute-start(bf16[6,2048]{0,1:T(8,128)(2,1)S(1)} %add_convert_fusion.9), channel_id=1, source_target_pairs={{2,0},{4,2},{6,4},{8,6},{10,8},{12,10},{14,12},{16,14},{18,16},{20... | collective-permute-start | bytes 73736 | tf_op jit(solution)/shard_map/ppermute | solution.py:10
  1039.3 11.9 copy-start.58
  1053.8 14.6 %collective-permute-start.22 = (bf16[128,2048]{1,0:T(8,128)(2,1)}, bf16[128,2048]{1,0:T(8,128)(2,1)}, u32[]{:S(2)}, u32[]{:S(2)}) collective-permute-start(bf16[128,2048]{1,0:T(8,128)(2,1)} %get-tuple-element.1093), channel_id=1, source_target_pairs={{32,0},{64,32},{96,64},{128,96},{160,128},{192,160},{224,192},{33,... | collective-permute-start | bytes 1572872 | tf_op jit(solution)/shard_map/ppermute | solution.py:10
  1068.4 311.9 %all-reduce.27.cloned.1.call-start = ((), (), s32[]{:S(2)}) async-start(), calls=%async_computation.9 | async-start | bytes 196608 | tf_op jit(solution)/shard_map/psum | solution.py:210
  1087.2 4.1 copy-start.2
  1090.0 149.2 %collective-permute-start.23 = (bf16[127,2048]{0,1:T(8,128)(2,1)}, bf16[127,2048]{0,1:T(8,128)(2,1)}, u32[]{:S(2)}, u32[]{:S(2)}) collective-permute-start(bf16[127,2048]{0,1:T(8,128)(2,1)} %bitcast.351), channel_id=1, source_target_pairs={{2,0},{4,2},{6,4},{8,6},{10,8},{12,10},{14,12},{16,14},{18,16},{20... | collective-permute-start | bytes 1560584 | tf_op jit(solution)/shard_map/ppermute | solution.py:10
  1248.0 5.9 copy-start.50
  1266.2 11.1 collective-permute-start.24
  (17 other events, 34.6 us)
Sparse Core Ops, SparseCore 0:
  9.8 16.9 all-gather.10
  29.2 127.3 all-gather.26
  235.9 55.9 all-gather.12
  361.1 63.2 all-gather.14
  493.1 63.9 all-gather.16
  626.2 64.8 all-gather.18
  760.0 63.8 all-gather.20
  937.9 16.6 all-gather.22
  1068.5 15.4 all-gather.24
  1268.5 111.7 all-reduce.26
where the time goes:
time: 1400 us; the launch traced here: 1390 us
  waiting for transfers between devices  826 us (59%)
  local copies, waits for them, and re-layouts  195 us (14%)
  other arithmetic  189 us (14%)
  blocking collectives  81.3 us (6%)
  starting transfers between devices  45.8 us (3%)
  matrix products  32.7 us (2%)
  between operations  15.6 us (1%)
    all_gather x8, waiting for transfers between devices, dense_grad(): piece = lax.all_gather(incoming, 'tp', axis=1, tiled=True)  330 us
    ppermute x25, waiting for transfers between devices, passed_along(): return lax.ppermute(array, axis, pairs)  327 us
    psum x1, waiting for transfers between devices, per_device(): lax.psum(short_local.astype(jnp.bfloat16), 'seq').astype(jnp.float32)  99.8 us
    reduce_sum x10, other arithmetic, spread_back(): jnp.sum(weights[offset][:, None, :] * feature_grads[:, offset:offset + ro...  88.6 us
    psum x1, blocking collectives, per_device(): lax.psum(long_local.astype(jnp.bfloat16), 'seq').astype(jnp.float32)  77.1 us
    all_gather x1, waiting for transfers between devices, per_device(): columns = lax.all_gather(out_weights[0], 'seq', axis=1, tiled=True)  68.1 us
    another operation x46, local copies, waits for them, and re-layouts  50.6 us
    ppermute x25, starting transfers between devices, passed_along(): return lax.ppermute(array, axis, pairs)  45.4 us
  transfers between devices with their start and end apart: 35, of which 32 were waited for; matrix products, arithmetic and copies ran while one was open for 12% of the time, Pallas kernels for 0%

commit v1 on v0

--- a/solution.py
+++ b/solution.py
@@ -183,7 +183,9 @@
     groups = filters.shape[0]
     saved_state = recompute(layer_inputs[0], weights, filters)
     features, padded, reversed_band, mixed_rows, source = saved_state
-    columns = lax.all_gather(out_weights[0], "seq", axis=1, tiled=True)
+    columns = jnp.concatenate(
+        lax.all_to_all(jnp.stack([out_weights[0]] * lax.axis_size("seq")), "seq", 0, 0), axis=1
+    )
     incoming = out_grad
     input_result = jnp.zeros_like(out_grad)
     dense_kept = jnp.zeros(out_grad.shape, jnp.bfloat16)

time: 1400 us -> 1560 us (1.11)
  waiting for transfers between devices: 826 us -> 954 us
  local copies, waits for them, and re-layouts: 195 us -> 223 us
    all_to_all x0 -> x1, waiting for transfers between devices: none -> 123 us  [per_device(): lax.all_to_all(jnp.stack([out_weights[0]] * lax.axis_size('seq')), 'seq',...]
    ppermute x25, waiting for transfers between devices: 327 us -> 421 us  [passed_along(): return lax.ppermute(array, axis, pairs)]
    all_gather x1 -> x0, waiting for transfers between devices: 68.1 us -> none  [per_device(): columns = lax.all_gather(out_weights[0], 'seq', axis=1, tiled=True)]
    all_to_all x0 -> x1, local copies, waits for them, and re-layouts: none -> 21.6 us  [per_device(): lax.all_to_all(jnp.stack([out_weights[0]] * lax.axis_size('seq')), 'seq',...]
    all_gather x8, waiting for transfers between devices: 330 us -> 313 us  [dense_grad(): piece = lax.all_gather(incoming, 'tp', axis=1, tiled=True)]
    another operation x46 -> x47, local copies, waits for them, and re-layouts: 50.6 us -> 56.4 us
  transfers between devices with their start and end apart: 35 -> 35, of which waited for: 32 -> 33; matrix products, arithmetic and copies ran while one was open for 12% -> 12% of each run, Pallas kernels for 0% -> 0%
where the time goes in v1:
time: 1560 us; the launch traced here: 1550 us
  waiting for transfers between devices  954 us (61%)
  local copies, waits for them, and re-layouts  223 us (14%)
  other arithmetic  189 us (12%)
  blocking collectives  81.3 us (5%)
  starting transfers between devices  57.8 us (4%)
  matrix products  29.5 us (2%)
    ppermute x25, waiting for transfers between devices, passed_along(): return lax.ppermute(array, axis, pairs)  421 us
    all_gather x8, waiting for transfers between devices, dense_grad(): piece = lax.all_gather(incoming, 'tp', axis=1, tiled=True)  313 us
    all_to_all x1, waiting for transfers between devices, per_device(): lax.all_to_all(jnp.stack([out_weights[0]] * lax.axis_size('seq')), 'seq',...  123 us
    psum x1, waiting for transfers between devices, per_device(): lax.psum(short_local.astype(jnp.bfloat16), 'seq').astype(jnp.float32)  96.5 us
    reduce_sum x10, other arithmetic, spread_back(): jnp.sum(weights[offset][:, None, :] * feature_grads[:, offset:offset + ro...  88.7 us
    psum x1, blocking collectives, per_device(): lax.psum(long_local.astype(jnp.bfloat16), 'seq').astype(jnp.float32)  77.1 us
    another operation x46, local copies, waits for them, and re-layouts  50.5 us
    ppermute x25, starting transfers between devices, passed_along(): return lax.ppermute(array, axis, pairs)  50 us
  transfers between devices with their start and end apart: 35, of which 33 were waited for; matrix products, arithmetic and copies ran while one was open for 12% of the time, Pallas kernels for 0%

profile of v1, /device:TPU:32, one launch (start us, length us, event | category | flops | bytes accessed | tf_op | source)
XLA Modules:
  0.0 1551.5 jit_solution(1414279517346782488)
XLA Ops:
  35.5 13.0 tile.10
  55.6 12.6 copy.354
  75.1 98.5 %collective-permute-done = bf16[6,2048]{1,0:T(8,128)(2,1)S(1)} collective-permute-done((bf16[6,2048]{1,0:T(8,128)(2,1)S(1)}, bf16[6,2048]{1,0:T(8,128)(2,1)S(1)}, u32[]{:S(2)}, u32[]{:S(2)}) %collective-permute-start) | collective-permute-done | bytes 24608 | tf_op jit(solution)/shard_map/ppermute | solution.py:10
  199.6 122.6 %all-to-all-done = bf16[16,2048,256]{2,1,0:T(8,128)(2,1)} async-done(((bf16[16,2048,256]{2,1,0:T(8,128)(2,1)}), bf16[16,2048,256]{2,1,0:T(8,128)(2,1)}, u32[]{:S(2)}, u32[]{:S(2)}) %all-to-all-start) | async-done | bytes 16777248 | tf_op jit(solution)/shard_map/all_to_all | solution.py:187
  322.1 21.6 %copy.274 = bf16[16,2048,256]{1,2,0:T(8,128)(2,1)} copy(bf16[16,2048,256]{2,1,0:T(8,128)(2,1)} %all-to-all-done) | data formatting | bytes 33554432 | tf_op jit(solution)/shard_map/all_to_all | solution.py:187
  399.1 12.2 collective-permute-done.3
  416.2 10.0 collective-permute-done.4
  426.4 53.1 %all-gather.11.cloned.1.call-done = bf16[128,4096]{1,0:T(8,128)(2,1)} async-done(((bf16[128,2048]{1,0:T(8,128)(2,1)}), bf16[128,4096]{1,0:T(8,128)(2,1)}) %all-gather.11.cloned.1.call-update) | async-done | bytes 1048592 | tf_op jit(solution)/shard_map/all_gather | solution.py:120
  485.4 14.7 collective-permute-done.5
  506.3 9.7 multiply_reduce_fusion.104
  517.6 13.9 collective-permute-done.6
  536.1 12.0 collective-permute-done.7
  548.1 59.9 %all-gather.13.cloned.1.call-done = bf16[128,4096]{1,0:T(8,128)(2,1)} async-done(((bf16[128,2048]{1,0:T(8,128)(2,1)}), bf16[128,4096]{1,0:T(8,128)(2,1)}) %all-gather.13.cloned.1.call-update) | async-done | bytes 1048592 | tf_op jit(solution)/shard_map/all_gather | solution.py:120
  613.9 14.7 collective-permute-done.8
  634.9 9.7 multiply_reduce_fusion.98
  646.2 13.9 collective-permute-done.9
  664.7 12.0 collective-permute-done.10
  676.7 60.7 %all-gather.15.cloned.1.call-done = bf16[128,4096]{1,0:T(8,128)(2,1)} async-done(((bf16[128,2048]{1,0:T(8,128)(2,1)}), bf16[128,4096]{1,0:T(8,128)(2,1)}) %all-gather.15.cloned.1.call-update) | async-done | bytes 1048592 | tf_op jit(solution)/shard_map/all_gather | solution.py:120
  743.5 14.7 collective-permute-done.11
  764.4 9.7 multiply_reduce_fusion.92
  775.8 13.9 collective-permute-done.12
  794.2 12.0 collective-permute-done.13
  806.3 61.5 %all-gather.17.cloned.1.call-done = bf16[128,4096]{1,0:T(8,128)(2,1)} async-done(((bf16[128,2048]{1,0:T(8,128)(2,1)}), bf16[128,4096]{1,0:T(8,128)(2,1)}) %all-gather.17.cloned.1.call-update) | async-done | bytes 1048592 | tf_op jit(solution)/shard_map/all_gather | solution.py:120
  873.6 14.7 collective-permute-done.14
  894.6 9.7 multiply_reduce_fusion.86
  905.9 13.9 collective-permute-done.15
  924.5 12.0 collective-permute-done.16
  936.5 60.6 %all-gather.19.cloned.1.call-done = bf16[128,4096]{1,0:T(8,128)(2,1)} async-done(((bf16[128,2048]{1,0:T(8,128)(2,1)}), bf16[128,4096]{1,0:T(8,128)(2,1)}) %all-gather.19.cloned.1.call-update) | async-done | bytes 1048592 | tf_op jit(solution)/shard_map/all_gather | solution.py:120
  1002.9 14.7 collective-permute-done.17
  1023.9 9.7 multiply_reduce_fusion.80
  1035.2 13.9 collective-permute-done.18
  1053.7 53.6 %collective-permute-done.19 = bf16[128,2048]{1,0:T(8,128)(2,1)} collective-permute-done((bf16[128,2048]{1,0:T(8,128)(2,1)}, bf16[128,2048]{1,0:T(8,128)(2,1)}, u32[]{:S(2)}, u32[]{:S(2)}) %collective-permute-start.19) | collective-permute-done | bytes 524320 | tf_op jit(solution)/shard_map/ppermute | solution.py:10
  1107.4 16.7 %all-gather.21.cloned.1.call-done = bf16[128,4096]{1,0:T(8,128)(2,1)} async-done(((bf16[128,2048]{1,0:T(8,128)(2,1)}), bf16[128,4096]{1,0:T(8,128)(2,1)}) %all-gather.21.cloned.1.call-update) | async-done | bytes 1048592 | tf_op jit(solution)/shard_map/all_gather | solution.py:120
  1124.1 14.4 conditional.42
  1124.4 9.7 fusion.9
  1141.1 14.7 collective-permute-done.20
  1157.2 13.0 conditional.43
  1173.0 9.7 multiply_reduce_fusion.74
  1184.3 13.9 collective-permute-done.21
  1199.3 20.9 %conditional.44 = (bf16[128,2048]{1,0:T(8,128)(2,1)}) conditional(s32[]{:T(128)} %convert_element_type.283, () %tuple.217, (bf16[128,2048]{1,0:T(8,128)(2,1)}, f32[7,3,2048]{2,1,0:T(4,128)S(1)}, f32[3,128,2048]{1,2,0:T(8,128)}, f32[6,2048]{0,1:T(8,128)}) %tuple.258), branch_computations={%region_125.126_spmd, %region_126.134_spmd} | conditional | flops 11796480 | bytes 26026020 | solution.py:175
  1205.7 11.9 multiply_reduce_fusion.47
  1222.1 12.7 collective-permute-done.22
  1265.5 17.8 %copy.355 = f32[128,128,256]{0,2,1:T(8,128)} copy(f32[128,128,256]{2,1,0:T(8,128)} %fusion.30) | data formatting | bytes 33554432 | tf_op jit(solution)/shard_map/reshape | solution.py:29
  1283.3 13.3 pad.28
  1296.6 17.5 %reshape.212 = f32[128,128,257]{0,2,1:T(8,128)} reshape(f32[128,32896]{0,1:T(8,128)} %pad.28) | data formatting | bytes 33685504 | tf_op jit(solution)/shard_map/reshape | solution.py:31
  1324.2 77.1 %psum.15 = bf16[1,128,128]{1,2,0:T(8,128)(2,1)} all-reduce(bf16[1,128,128]{1,2,0:T(8,128)(2,1)} %bitcast.403), channel_id=1, replica_groups=mesh['pipe'=8,'seq'=16,'tp'=2] {'seq'}, use_global_device_ids=true, to_apply=%region_162.163 | all-reduce | flops 16384 | bytes 65536 | tf_op jit(solution)/shard_map/psum | solution.py:213
  1422.5 9.4 multiply_reduce_fusion.68
  1446.5 96.5 %all-reduce.27.cloned.1.call-done = bf16[1,7,3,2048]{3,1,2,0:T(8,128)(2,1)} async-done(((bf16[1,7,3,2048]{3,1,2,0:T(8,128)(2,1)}), bf16[1,7,3,2048]{3,1,2,0:T(8,128)(2,1)}) %all-reduce.27.cloned.1.call-update) | async-done | bytes 86032 | tf_op jit(solution)/shard_map/psum | solution.py:212
  (286 shorter events, 378.0 us)
Async XLA Ops:
  7.2 5.8 copy-start.52
  18.9 11.9 copy-start.65
  18.9 303.2 %all-to-all-start = ((bf16[16,2048,256]{2,1,0:T(8,128)(2,1)}), bf16[16,2048,256]{2,1,0:T(8,128)(2,1)}, u32[]{:S(2)}, u32[]{:S(2)}) async-start(bf16[16,2048,256]{2,1,0:T(8,128)(2,1)} %stack.111), calls=%async_computation | async-start | bytes 33554432 | tf_op jit(solution)/shard_map/all_to_all | solution.py:187
  26.1 317.7 %all-gather.9.cloned.1.call-start = ((), (), s32[]{:S(2)}) async-start(), calls=%async_computation.2 | async-start | bytes 1572864 | tf_op jit(solution)/shard_map/all_gather | solution.py:120
  26.9 452.6 %all-gather.11.cloned.1.call-start = ((), (), s32[]{:S(2)}) async-start(), calls=%async_computation.3 | async-start | bytes 1572864 | tf_op jit(solution)/shard_map/all_gather | solution.py:120
  26.9 146.7 %collective-permute-start = (bf16[6,2048]{1,0:T(8,128)(2,1)S(1)}, bf16[6,2048]{1,0:T(8,128)(2,1)S(1)}, u32[]{:S(2)}, u32[]{:S(2)}) collective-permute-start(bf16[6,2048]{1,0:T(8,128)(2,1)S(1)} %slice.757), channel_id=1, source_target_pairs={{0,2},{2,4},{4,6},{6,8},{8,10},{10,12},{12,14},{14,16},{16,18},{18... | collective-permute-start | bytes 73736 | tf_op jit(solution)/shard_map/ppermute | solution.py:10
  55.6 12.6 copy-start.64
  181.7 7.7 copy-start.32
  350.9 16.9 %collective-permute-start.1 = (bf16[127,2048]{0,1:T(8,128)(2,1)}, bf16[127,2048]{0,1:T(8,128)(2,1)}, u32[]{:S(2)}, u32[]{:S(2)}) collective-permute-start(bf16[127,2048]{0,1:T(8,128)(2,1)} %slice.773), channel_id=1, source_target_pairs={{0,2},{2,4},{4,6},{6,8},{8,10},{10,12},{12,14},{14,16},{16,18},{18... | collective-permute-start | bytes 1560584 | tf_op jit(solution)/shard_map/ppermute | solution.py:10
  357.9 14.7 collective-permute-start.2
  373.6 9.6 slice-start
  376.1 7.1 copy-start.1
  376.1 7.1 slice-start.1
  397.8 13.5 collective-permute-start.3
  413.2 13.1 collective-permute-start.4
  426.3 181.7 %all-gather.13.cloned.1.call-start = ((), (), s32[]{:S(2)}) async-start(), calls=%async_computation.4 | async-start | bytes 1572864 | tf_op jit(solution)/shard_map/all_gather | solution.py:120
  484.1 16.0 %collective-permute-start.5 = (bf16[127,2048]{0,1:T(8,128)(2,1)S(1)}, bf16[127,2048]{0,1:T(8,128)(2,1)S(1)}, u32[]{:S(2)}, u32[]{:S(2)}) collective-permute-start(bf16[127,2048]{0,1:T(8,128)(2,1)S(1)} %bitcast.395), channel_id=1, source_target_pairs={{2,0},{4,2},{6,4},{8,6},{10,8},{12,10},{14,12},{16,14},{18,16},{20... | collective-permute-start | bytes 1560584 | tf_op jit(solution)/shard_map/ppermute | solution.py:10
  503.5 2.8 copy-start.8
  516.3 15.2 collective-permute-start.6
  533.4 14.6 collective-permute-start.7
  548.1 189.4 %all-gather.15.cloned.1.call-start = ((), (), s32[]{:S(2)}) async-start(), calls=%async_computation.5 | async-start | bytes 1572864 | tf_op jit(solution)/shard_map/all_gather | solution.py:120
  612.6 16.0 %collective-permute-start.8 = (bf16[127,2048]{0,1:T(8,128)(2,1)S(1)}, bf16[127,2048]{0,1:T(8,128)(2,1)S(1)}, u32[]{:S(2)}, u32[]{:S(2)}) collective-permute-start(bf16[127,2048]{0,1:T(8,128)(2,1)S(1)} %bitcast.396), channel_id=1, source_target_pairs={{2,0},{4,2},{6,4},{8,6},{10,8},{12,10},{14,12},{16,14},{18,16},{20... | collective-permute-start | bytes 1560584 | tf_op jit(solution)/shard_map/ppermute | solution.py:10
  632.0 2.8 copy-start.11
  644.9 15.2 collective-permute-start.9
  662.1 14.6 collective-permute-start.10
  676.7 191.1 %all-gather.17.cloned.1.call-start = ((), (), s32[]{:S(2)}) async-start(), calls=%async_computation.6 | async-start | bytes 1572864 | tf_op jit(solution)/shard_map/all_gather | solution.py:120
  742.2 16.0 %collective-permute-start.11 = (bf16[127,2048]{0,1:T(8,128)(2,1)S(1)}, bf16[127,2048]{0,1:T(8,128)(2,1)S(1)}, u32[]{:S(2)}, u32[]{:S(2)}) collective-permute-start(bf16[127,2048]{0,1:T(8,128)(2,1)S(1)} %bitcast.397), channel_id=1, source_target_pairs={{2,0},{4,2},{6,4},{8,6},{10,8},{12,10},{14,12},{16,14},{18,16},{20... | collective-permute-start | bytes 1560584 | tf_op jit(solution)/shard_map/ppermute | solution.py:10
  774.5 15.2 collective-permute-start.12
  791.6 14.6 collective-permute-start.13
  806.2 190.8 %all-gather.19.cloned.1.call-start = ((), (), s32[]{:S(2)}) async-start(), calls=%async_computation.7 | async-start | bytes 1572864 | tf_op jit(solution)/shard_map/all_gather | solution.py:120
  872.3 16.0 %collective-permute-start.14 = (bf16[127,2048]{0,1:T(8,128)(2,1)S(1)}, bf16[127,2048]{0,1:T(8,128)(2,1)S(1)}, u32[]{:S(2)}, u32[]{:S(2)}) collective-permute-start(bf16[127,2048]{0,1:T(8,128)(2,1)S(1)} %bitcast.398), channel_id=1, source_target_pairs={{2,0},{4,2},{6,4},{8,6},{10,8},{12,10},{14,12},{16,14},{18,16},{20... | collective-permute-start | bytes 1560584 | tf_op jit(solution)/shard_map/ppermute | solution.py:10
  904.6 15.2 collective-permute-start.15
  921.8 14.6 collective-permute-start.16
  936.5 187.6 %all-gather.21.cloned.1.call-start = ((), (), s32[]{:S(2)}) async-start(), calls=%async_computation.8 | async-start | bytes 1572864 | tf_op jit(solution)/shard_map/all_gather | solution.py:120
  1001.6 16.0 %collective-permute-start.17 = (bf16[127,2048]{0,1:T(8,128)(2,1)S(1)}, bf16[127,2048]{0,1:T(8,128)(2,1)S(1)}, u32[]{:S(2)}, u32[]{:S(2)}) collective-permute-start(bf16[127,2048]{0,1:T(8,128)(2,1)S(1)} %bitcast.399), channel_id=1, source_target_pairs={{2,0},{4,2},{6,4},{8,6},{10,8},{12,10},{14,12},{16,14},{18,16},{20... | collective-permute-start | bytes 1560584 | tf_op jit(solution)/shard_map/ppermute | solution.py:10
  1033.9 15.2 collective-permute-start.18
  1051.0 56.3 %collective-permute-start.19 = (bf16[128,2048]{1,0:T(8,128)(2,1)}, bf16[128,2048]{1,0:T(8,128)(2,1)}, u32[]{:S(2)}, u32[]{:S(2)}) collective-permute-start(bf16[128,2048]{1,0:T(8,128)(2,1)} %get-tuple-element.1183), channel_id=1, source_target_pairs={{32,0},{64,32},{96,64},{128,96},{160,128},{192,160},{224,192},{33,... | collective-permute-start | bytes 1572872 | tf_op jit(solution)/shard_map/ppermute | solution.py:10
  1107.3 143.1 %all-gather.23.cloned.1.call-start = ((), (), s32[]{:S(2)}) async-start(), calls=%async_computation.9 | async-start | bytes 1572864 | tf_op jit(solution)/shard_map/all_gather | solution.py:120
  1139.8 16.0 %collective-permute-start.20 = (bf16[127,2048]{0,1:T(8,128)(2,1)S(1)}, bf16[127,2048]{0,1:T(8,128)(2,1)S(1)}, u32[]{:S(2)}, u32[]{:S(2)}) collective-permute-start(bf16[127,2048]{0,1:T(8,128)(2,1)S(1)} %bitcast.400), channel_id=1, source_target_pairs={{2,0},{4,2},{6,4},{8,6},{10,8},{12,10},{14,12},{16,14},{18,16},{20... | collective-permute-start | bytes 1560584 | tf_op jit(solution)/shard_map/ppermute | solution.py:10
  1170.1 2.8 copy-start.23
  1183.0 15.2 collective-permute-start.21
  1205.7 11.9 copy-start.59
  1220.2 14.6 collective-permute-start.22
  1234.8 308.3 %all-reduce.27.cloned.1.call-start = ((), (), s32[]{:S(2)}) async-start(), calls=%async_computation.10 | async-start | bytes 196608 | tf_op jit(solution)/shard_map/psum | solution.py:212
  1253.3 4.0 copy-start.2
  1256.1 149.1 %collective-permute-start.23 = (bf16[127,2048]{0,1:T(8,128)(2,1)}, bf16[127,2048]{0,1:T(8,128)(2,1)}, u32[]{:S(2)}, u32[]{:S(2)}) collective-permute-start(bf16[127,2048]{0,1:T(8,128)(2,1)} %bitcast.354), channel_id=1, source_target_pairs={{2,0},{4,2},{6,4},{8,6},{10,8},{12,10},{14,12},{16,14},{18,16},{20... | collective-permute-start | bytes 1560584 | tf_op jit(solution)/shard_map/ppermute | solution.py:10
  1414.0 5.9 copy-start.50
  1432.3 11.1 collective-permute-start.24
  (18 other events, 37.5 us)
Sparse Core Ops, SparseCore 0:
  28.8 17.0 all-gather.8
  426.4 52.9 all-gather.10
  548.2 59.8 all-gather.12
  676.8 60.5 all-gather.14
  806.3 61.3 all-gather.16
  936.6 60.4 all-gather.18
  1107.4 16.5 all-gather.20
  1234.9 15.4 all-gather.22
  1434.6 108.4 all-reduce.26
